TPU v7x, 512 devices: a whole 4x4x16 slice. The times are simulated.
512 devices in a mesh: pipe: 32 (over y, x, core), dp: 16 (over z).
Axes of the slice: x: 4, y: 4, z: 16, core: 2. Of those that a mesh axis runs over, the one named last changes fastest.
Arguments:
- x_saved: bfloat16 [32, 4096, 1024], P('pipe', 'dp'), may hold values from -6 to 6
- up_weights: bfloat16 [32, 1024, 2048], P('pipe', 'dp'), may hold values from -0.1875 to 0.1875
- down_weights: bfloat16 [32, 2048, 1024], P('pipe', 'dp'), may hold values from -0.125 to 0.125
- norm_gain: float32 [32, 1024], P('pipe'), may hold values from 0.1 to 1.9
- layer_scale: float32 [32, 1024], P('pipe'), may hold values from 0.1 to 1
- cotangent: bfloat16 [4096, 1024], P('dp'), may hold values from -0.119628906 to 0.119628906
- lengths: int32 [16, 2], P('dp'), may hold values from 1 to 128, 160 in all within a row
Outputs:
- weight_grad: bfloat16 [32, 2048, 1024], P('pipe', 'dp')
- gain_grad: float32 [32, 1024], P('pipe')
- scale_grad: float32 [32, 1024], P('pipe')
All inputs are finite; a program needn't handle non-finite values.
Results may differ from a plain program's by a relative error of at most 0.04.
Values may be sent and summed in bfloat16 or wider, within the bound.
A program may use at most 64 MiB of HBM per device.

v0:
```python
import jax
import jax.numpy as jnp
from jax import lax
from jax.sharding import PartitionSpec as P

epsilon = 1e-06


def passed_along(block, axis, distance):
    devices = range(lax.axis_size(axis))
    route = [(i - distance, i) for i in devices if i - distance in devices]
    return lax.ppermute(block, axis, route)


def gelu_tanh(values):
    return jax.nn.gelu(values, approximate=True)


def layer_back(x_rows, incoming, up_weight, down_weight, gain_vec, scale_vec):
    x_float = x_rows.astype(jnp.float32)
    inverse = lax.rsqrt(jnp.mean(x_float * x_float, axis=-1, keepdims=True) + epsilon)
    unit = x_float * inverse
    normed = (unit * gain_vec).astype(jnp.bfloat16)
    hidden = jnp.dot(normed, up_weight, preferred_element_type=jnp.float32)
    active, gelu_back = jax.vjp(gelu_tanh, hidden)
    act = active.astype(jnp.bfloat16)
    branch = jnp.dot(act, down_weight, preferred_element_type=jnp.float32)
    upper = incoming.astype(jnp.float32)
    scale_part = jnp.sum(upper * branch, axis=0)
    branch_grad = (upper * scale_vec).astype(jnp.bfloat16)
    act_grad = jnp.dot(branch_grad, down_weight.T, preferred_element_type=jnp.float32)
    hidden_grad = gelu_back(act_grad)[0].astype(jnp.bfloat16)
    normed_grad = jnp.dot(hidden_grad, up_weight.T, preferred_element_type=jnp.float32)
    gain_part = jnp.sum(normed_grad * unit, axis=0)
    unit_grad = normed_grad * gain_vec
    back_rows = (
        upper + inverse * (unit_grad - unit * jnp.mean(unit_grad * unit, axis=-1, keepdims=True))
    ).astype(jnp.bfloat16)
    return (act, branch_grad, back_rows, gain_part, scale_part)


def shards(x_saved, up_weights, down_weights, norm_gain, layer_scale, cotangent, lengths):
    section_count = lax.axis_size("pipe")
    section_index = lax.axis_index("pipe")
    up_full, down_full = (
        lax.all_gather(up_weights, "dp", axis=1, tiled=True),
        lax.all_gather(down_weights, "dp", axis=1, tiled=True),
    )
    up_weight = up_full[0]
    down_weight = down_full[0]
    x_rows = x_saved[0]
    gain_vec = norm_gain[0]
    scale_vec = layer_scale[0]
    row_count = x_rows.shape[0]
    width = x_rows.shape[1]
    hidden_width = up_weight.shape[1]
    batches = lengths.shape[1]
    slot_rows = row_count // batches
    row_ids = jnp.arange(row_count, dtype=jnp.int32)
    position = row_ids % slot_rows
    owner = row_ids // slot_rows
    match = owner[:, None] == jnp.arange(batches, dtype=jnp.int32)[None, :]
    valid_len = jnp.sum(jnp.where(match, lengths[0][None, :], 0), axis=1)
    start_grad = jnp.where((position < valid_len)[:, None], cotangent, jnp.zeros_like(cotangent))
    pieces = 2 * batches
    piece_rows = row_count // pieces

    def step(step_index, carry):
        received, act_store, grad_store, acc_gain, acc_scale = carry
        piece_index = step_index - (section_count - 1 - section_index)
        working = jnp.logical_and(piece_index >= 0, piece_index < pieces)
        clamped = jnp.clip(piece_index, 0, pieces - 1)
        row_start = clamped * piece_rows
        x_piece = lax.dynamic_slice_in_dim(x_rows, row_start, piece_rows, 0)
        start_piece = lax.dynamic_slice_in_dim(start_grad, row_start, piece_rows, 0)
        incoming = jnp.where(section_index == section_count - 1, start_piece, received)

        def compute(unused):
            act, branch_grad, back_rows, gain_part, scale_part = layer_back(
                x_piece, incoming, up_weight, down_weight, gain_vec, scale_vec
            )
            new_act = lax.dynamic_update_slice_in_dim(act_store, act, row_start, 0)
            new_grad = lax.dynamic_update_slice_in_dim(grad_store, branch_grad, row_start, 0)
            return (back_rows, new_act, new_grad, acc_gain + gain_part, acc_scale + scale_part)

        def waiting(unused):
            return (jnp.zeros_like(received), act_store, grad_store, acc_gain, acc_scale)

        back_rows, act_store, grad_store, acc_gain, acc_scale = lax.cond(
            working, compute, waiting, 0
        )
        received = passed_along(back_rows, "pipe", -1)
        return (received, act_store, grad_store, acc_gain, acc_scale)

    start_carry = (
        jnp.zeros((piece_rows, width), jnp.bfloat16),
        jnp.zeros((row_count, hidden_width), jnp.bfloat16),
        jnp.zeros((row_count, width), jnp.bfloat16),
        jnp.zeros((width,), jnp.float32),
        jnp.zeros((width,), jnp.float32),
    )
    received, act_store, grad_store, acc_gain, acc_scale = lax.fori_loop(
        0, pieces + section_count - 1, step, start_carry
    )
    partial_grad = lax.dot_general(
        act_store, grad_store, (((0,), (0,)), ((), ())), preferred_element_type=jnp.float32
    ).astype(jnp.bfloat16)
    weight_part = lax.psum_scatter(partial_grad, "dp", scatter_dimension=0, tiled=True).astype(
        jnp.float32
    )
    gain_total, scale_total = lax.psum((acc_gain, acc_scale), "dp")
    return (weight_part.astype(jnp.bfloat16)[None], gain_total[None], scale_total[None])


def solution(mesh):
    return jax.shard_map(
        shards,
        mesh=mesh,
        in_specs=(
            P("pipe", "dp", None),
            P("pipe", "dp", None),
            P("pipe", "dp", None),
            P("pipe", None),
            P("pipe", None),
            P("dp", None),
            P("dp", None),
        ),
        out_specs=(P("pipe", "dp", None), P("pipe", None), P("pipe", None)),
        check_vma=False,
    )
```

profile of v0, /device:TPU:12, one launch (start us, length us, event | category | flops | bytes accessed | tf_op | source)
XLA Modules:
  0.0 945.7 jit_solution(14448005676773442132)
XLA Ops:
  10.6 81.8 %all-gather.5.cloned.1.call-done = bf16[1,1024,2048]{2,1,0:T(8,128)(2,1)} async-done(((bf16[1,64,2048]{2,1,0:T(8,128)(2,1)}), bf16[1,1024,2048]{2,1,0:T(8,128)(2,1)}) %all-gather.5.cloned.1.call-update) | async-done | bytes 4194320 | tf_op jit(solution)/shard_map/all_gather | solution.py:46
  92.4 76.5 %all-gather.3.cloned.1.call-done = bf16[1,2048,1024]{2,1,0:T(8,128)(2,1)} async-done(((bf16[1,128,1024]{2,1,0:T(8,128)(2,1)}), bf16[1,2048,1024]{2,1,0:T(8,128)(2,1)}) %all-gather.3.cloned.1.call-update) | async-done | bytes 4194320 | tf_op jit(solution)/shard_map/all_gather | solution.py:47
  170.0 605.6 %while.23 = (s32[]{:T(128)}, bf16[64,1024]{1,0:T(8,128)(2,1)S(1)}, bf16[256,2048]{1,0:T(8,128)(2,1)S(1)}, bf16[256,1024]{1,0:T(8,128)(2,1)}, f32[1024]{0:T(1024)...) while((s32[]{:T(128)}, bf16[64,1024]{1,0:T(8,128)(2,1)S(1)}, ...), condition=%wide.region_8.9_spmd, body=%wide.region_1.8_spmd.sunk | while | flops 1080885248 | bytes 23421764 | solution.py:102
  174.5 3.8 collective-permute-start
  180.8 3.8 collective-permute-start
  187.2 3.8 collective-permute-start
  193.5 3.8 collective-permute-start
  199.8 3.8 collective-permute-start
  206.1 3.8 collective-permute-start
  212.9 3.3 collective-permute-start
  216.2 5.1 collective-permute-done
  223.3 6.5 collective-permute-done
  231.7 6.5 collective-permute-done
  240.2 6.5 collective-permute-done
  248.6 6.5 collective-permute-done
  257.0 6.5 collective-permute-done
  265.5 6.5 collective-permute-done
  273.9 6.5 collective-permute-done
  282.3 6.5 collective-permute-done
  290.7 6.5 collective-permute-done
  299.2 6.5 collective-permute-done
  307.6 227.4 %collective-permute-done = bf16[64,1024]{1,0:T(8,128)(2,1)S(1)} collective-permute-done((bf16[64,1024]{1,0:T(8,128)(2,1)S(1)}, bf16[64,1024]{1,0:T(8,128)(2,1)S(1)}, u32[]{:S(2)}, u32[]{:S(2)}) %collective-permute-start) | collective-permute-done | bytes 131104 | tf_op jit(solution)/shard_map/while/body/eval_jaxpr/ppermute | solution.py:12
  535.0 15.4 %conditional.2 = (bf16[64,1024]{1,0:T(8,128)(2,1)S(1)}, bf16[256,2048]{1,0:T(8,128)(2,1)S(1)}, bf16[256,1024]{1,0:T(8,128)(2,1)}, f32[1024]{0:T(1024)S(1)}, f32[1024]{0:T(1024)S(1)}) conditional(s32[]{:T(128)} %convert_element_type.134, (bf16[256,2048]{1,0:T(8,128)(2,1)S(1)}, bf16[256,1024]{1,0:T(8,128)(2,1)}, f32[1024]{0:T(1024)S(1)}, ...), branch_computations={%region_2.2_spmd, %region_3.7_spmd} | conditional | flops 1080885248 | bytes 22897106 | solution.py:89
  540.8 6.3 fusion.16
  552.4 6.5 collective-permute-done
  558.8 15.4 %conditional.2 = (bf16[64,1024]{1,0:T(8,128)(2,1)S(1)}, bf16[256,2048]{1,0:T(8,128)(2,1)S(1)}, bf16[256,1024]{1,0:T(8,128)(2,1)}, f32[1024]{0:T(1024)S(1)}, f32[1024]{0:T(1024)S(1)}) conditional(s32[]{:T(128)} %convert_element_type.134, (bf16[256,2048]{1,0:T(8,128)(2,1)S(1)}, bf16[256,1024]{1,0:T(8,128)(2,1)}, f32[1024]{0:T(1024)S(1)}, ...), branch_computations={%region_2.2_spmd, %region_3.7_spmd} | conditional | flops 1080885248 | bytes 22897106 | solution.py:89
  564.7 6.3 fusion.16
  576.2 6.4 collective-permute-done
  582.6 15.4 %conditional.2 = (bf16[64,1024]{1,0:T(8,128)(2,1)S(1)}, bf16[256,2048]{1,0:T(8,128)(2,1)S(1)}, bf16[256,1024]{1,0:T(8,128)(2,1)}, f32[1024]{0:T(1024)S(1)}, f32[1024]{0:T(1024)S(1)}) conditional(s32[]{:T(128)} %convert_element_type.134, (bf16[256,2048]{1,0:T(8,128)(2,1)S(1)}, bf16[256,1024]{1,0:T(8,128)(2,1)}, f32[1024]{0:T(1024)S(1)}, ...), branch_computations={%region_2.2_spmd, %region_3.7_spmd} | conditional | flops 1080885248 | bytes 22897106 | solution.py:89
  588.4 6.3 fusion.16
  599.9 6.5 collective-permute-done
  606.4 15.4 %conditional.2 = (bf16[64,1024]{1,0:T(8,128)(2,1)S(1)}, bf16[256,2048]{1,0:T(8,128)(2,1)S(1)}, bf16[256,1024]{1,0:T(8,128)(2,1)}, f32[1024]{0:T(1024)S(1)}, f32[1024]{0:T(1024)S(1)}) conditional(s32[]{:T(128)} %convert_element_type.134, (bf16[256,2048]{1,0:T(8,128)(2,1)S(1)}, bf16[256,1024]{1,0:T(8,128)(2,1)}, f32[1024]{0:T(1024)S(1)}, ...), branch_computations={%region_2.2_spmd, %region_3.7_spmd} | conditional | flops 1080885248 | bytes 22897106 | solution.py:89
  612.2 6.3 fusion.16
  626.3 19.2 %collective-permute-start = (bf16[64,1024]{1,0:T(8,128)(2,1)S(1)}, bf16[64,1024]{1,0:T(8,128)(2,1)S(1)}, u32[]{:S(2)}, u32[]{:S(2)}) collective-permute-start(bf16[64,1024]{1,0:T(8,128)(2,1)S(1)} %get-tuple-element.654), channel_id=1, source_target_pairs={{16,0},{32,16},{48,32},{64,48},{80,64},{96,80},{112,96},{128,112},... | collective-permute-start | bytes 393224 | tf_op jit(solution)/shard_map/while/body/eval_jaxpr/ppermute | solution.py:12
  648.0 3.8 collective-permute-start
  654.3 12.7 %collective-permute-start = (bf16[64,1024]{1,0:T(8,128)(2,1)S(1)}, bf16[64,1024]{1,0:T(8,128)(2,1)S(1)}, u32[]{:S(2)}, u32[]{:S(2)}) collective-permute-start(bf16[64,1024]{1,0:T(8,128)(2,1)S(1)} %get-tuple-element.654), channel_id=1, source_target_pairs={{16,0},{32,16},{48,32},{64,48},{80,64},{96,80},{112,96},{128,112},... | collective-permute-start | bytes 393224 | tf_op jit(solution)/shard_map/while/body/eval_jaxpr/ppermute | solution.py:12
  669.5 3.8 collective-permute-start
  675.9 17.3 %collective-permute-start = (bf16[64,1024]{1,0:T(8,128)(2,1)S(1)}, bf16[64,1024]{1,0:T(8,128)(2,1)S(1)}, u32[]{:S(2)}, u32[]{:S(2)}) collective-permute-start(bf16[64,1024]{1,0:T(8,128)(2,1)S(1)} %get-tuple-element.654), channel_id=1, source_target_pairs={{16,0},{32,16},{48,32},{64,48},{80,64},{96,80},{112,96},{128,112},... | collective-permute-start | bytes 393224 | tf_op jit(solution)/shard_map/while/body/eval_jaxpr/ppermute | solution.py:12
  695.7 3.8 collective-permute-start
  702.0 12.7 %collective-permute-start = (bf16[64,1024]{1,0:T(8,128)(2,1)S(1)}, bf16[64,1024]{1,0:T(8,128)(2,1)S(1)}, u32[]{:S(2)}, u32[]{:S(2)}) collective-permute-start(bf16[64,1024]{1,0:T(8,128)(2,1)S(1)} %get-tuple-element.654), channel_id=1, source_target_pairs={{16,0},{32,16},{48,32},{64,48},{80,64},{96,80},{112,96},{128,112},... | collective-permute-start | bytes 393224 | tf_op jit(solution)/shard_map/while/body/eval_jaxpr/ppermute | solution.py:12
  717.3 3.8 collective-permute-start
  723.6 19.5 %collective-permute-start = (bf16[64,1024]{1,0:T(8,128)(2,1)S(1)}, bf16[64,1024]{1,0:T(8,128)(2,1)S(1)}, u32[]{:S(2)}, u32[]{:S(2)}) collective-permute-start(bf16[64,1024]{1,0:T(8,128)(2,1)S(1)} %get-tuple-element.654), channel_id=1, source_target_pairs={{16,0},{32,16},{48,32},{64,48},{80,64},{96,80},{112,96},{128,112},... | collective-permute-start | bytes 393224 | tf_op jit(solution)/shard_map/while/body/eval_jaxpr/ppermute | solution.py:12
  745.6 5.9 collective-permute-start
  754.1 10.6 %collective-permute-start = (bf16[64,1024]{1,0:T(8,128)(2,1)S(1)}, bf16[64,1024]{1,0:T(8,128)(2,1)S(1)}, u32[]{:S(2)}, u32[]{:S(2)}) collective-permute-start(bf16[64,1024]{1,0:T(8,128)(2,1)S(1)} %get-tuple-element.654), channel_id=1, source_target_pairs={{16,0},{32,16},{48,32},{64,48},{80,64},{96,80},{112,96},{128,112},... | collective-permute-start | bytes 393224 | tf_op jit(solution)/shard_map/while/body/eval_jaxpr/ppermute | solution.py:12
  767.2 5.9 collective-permute-start
  775.6 4.3 convolution_convert_fusion
  779.9 29.2 %all-reduce = (f32[1,1024]{1,0:T(1,128)}, f32[1,1024]{1,0:T(1,128)}) all-reduce(f32[1,1024]{1,0:T(1,128)S(1)} %bitcast.24, f32[1,1024]{1,0:T(1,128)S(1)} %bitcast.23), channel_id=1, replica_groups=mesh['pipe'=32,'dp'=16] {'dp'}, use_global_device_ids=true, to_apply=%region_10.11 | all-reduce | flops 2048 | bytes 16384 | tf_op jit(solution)/shard_map/psum | solution.py:111
  809.1 130.1 %reduce-scatter.2.cloned.1.call-done = bf16[128,1024]{1,0:T(8,128)(2,1)} async-done(((bf16[2048,1024]{1,0:T(8,128)(2,1)}), bf16[128,1024]{1,0:T(8,128)(2,1)}) %reduce-scatter.2.cloned.1.call-update) | async-done | bytes 262160 | tf_op jit(solution)/shard_map/reduce_scatter | solution.py:108
  (173 shorter events, 122.7 us)
Async XLA Ops:
  7.2 85.2 %all-gather.5.cloned.1.call-start = ((), (), s32[]{:S(2)}) async-start(), calls=%async_computation.2 | async-start | bytes 4456448 | tf_op jit(solution)/shard_map/all_gather | solution.py:46
  7.9 161.0 %all-gather.3.cloned.1.call-start = ((), (), s32[]{:S(2)}) async-start(), calls=%async_computation.1 | async-start | bytes 4456448 | tf_op jit(solution)/shard_map/all_gather | solution.py:47
  8.6 930.5 %reduce-scatter.2.cloned.1.call-start = ((), (), s32[]{:S(2)}) async-start(), calls=%async_computation.3 | async-start | bytes 4456448 | tf_op jit(solution)/shard_map/reduce_scatter | solution.py:108
  170.1 4.4 collective-permute-start
  174.5 6.3 collective-permute-start
  180.8 6.3 collective-permute-start
  187.2 6.3 collective-permute-start
  193.5 6.3 collective-permute-start
  199.8 6.3 collective-permute-start
  206.1 6.8 collective-permute-start
  212.9 8.4 collective-permute-start
  221.4 8.4 collective-permute-start
  229.8 8.4 collective-permute-start
  238.2 8.4 collective-permute-start
  246.7 8.4 collective-permute-start
  255.1 8.4 collective-permute-start
  263.5 8.4 collective-permute-start
  272.0 8.4 collective-permute-start
  280.4 8.4 collective-permute-start
  288.8 8.4 collective-permute-start
  297.2 8.4 collective-permute-start
  305.7 229.3 %collective-permute-start = (bf16[64,1024]{1,0:T(8,128)(2,1)S(1)}, bf16[64,1024]{1,0:T(8,128)(2,1)S(1)}, u32[]{:S(2)}, u32[]{:S(2)}) collective-permute-start(bf16[64,1024]{1,0:T(8,128)(2,1)S(1)} %get-tuple-element.654), channel_id=1, source_target_pairs={{16,0},{32,16},{48,32},{64,48},{80,64},{96,80},{112,96},{128,112},... | collective-permute-start | bytes 393224 | tf_op jit(solution)/shard_map/while/body/eval_jaxpr/ppermute | solution.py:12
  535.0 5.8 copy-start
  535.0 5.8 copy-start.1
  535.0 5.8 copy-start.2
  550.4 8.4 collective-permute-start
  558.8 5.8 copy-start
  558.8 5.8 copy-start.1
  558.8 5.8 copy-start.2
  574.2 8.3 collective-permute-start
  582.6 5.8 copy-start.2
  598.0 8.4 collective-permute-start
  606.4 5.8 copy-start
  606.4 5.8 copy-start.1
  606.4 5.8 copy-start.2
  621.8 4.4 collective-permute-start
  626.3 21.7 %collective-permute-start = (bf16[64,1024]{1,0:T(8,128)(2,1)S(1)}, bf16[64,1024]{1,0:T(8,128)(2,1)S(1)}, u32[]{:S(2)}, u32[]{:S(2)}) collective-permute-start(bf16[64,1024]{1,0:T(8,128)(2,1)S(1)} %get-tuple-element.654), channel_id=1, source_target_pairs={{16,0},{32,16},{48,32},{64,48},{80,64},{96,80},{112,96},{128,112},... | collective-permute-start | bytes 393224 | tf_op jit(solution)/shard_map/while/body/eval_jaxpr/ppermute | solution.py:12
  648.0 6.3 collective-permute-start
  654.3 15.2 %collective-permute-start = (bf16[64,1024]{1,0:T(8,128)(2,1)S(1)}, bf16[64,1024]{1,0:T(8,128)(2,1)S(1)}, u32[]{:S(2)}, u32[]{:S(2)}) collective-permute-start(bf16[64,1024]{1,0:T(8,128)(2,1)S(1)} %get-tuple-element.654), channel_id=1, source_target_pairs={{16,0},{32,16},{48,32},{64,48},{80,64},{96,80},{112,96},{128,112},... | collective-permute-start | bytes 393224 | tf_op jit(solution)/shard_map/while/body/eval_jaxpr/ppermute | solution.py:12
  669.5 6.3 collective-permute-start
  675.9 19.8 %collective-permute-start = (bf16[64,1024]{1,0:T(8,128)(2,1)S(1)}, bf16[64,1024]{1,0:T(8,128)(2,1)S(1)}, u32[]{:S(2)}, u32[]{:S(2)}) collective-permute-start(bf16[64,1024]{1,0:T(8,128)(2,1)S(1)} %get-tuple-element.654), channel_id=1, source_target_pairs={{16,0},{32,16},{48,32},{64,48},{80,64},{96,80},{112,96},{128,112},... | collective-permute-start | bytes 393224 | tf_op jit(solution)/shard_map/while/body/eval_jaxpr/ppermute | solution.py:12
  695.7 6.3 collective-permute-start
  702.0 15.2 %collective-permute-start = (bf16[64,1024]{1,0:T(8,128)(2,1)S(1)}, bf16[64,1024]{1,0:T(8,128)(2,1)S(1)}, u32[]{:S(2)}, u32[]{:S(2)}) collective-permute-start(bf16[64,1024]{1,0:T(8,128)(2,1)S(1)} %get-tuple-element.654), channel_id=1, source_target_pairs={{16,0},{32,16},{48,32},{64,48},{80,64},{96,80},{112,96},{128,112},... | collective-permute-start | bytes 393224 | tf_op jit(solution)/shard_map/while/body/eval_jaxpr/ppermute | solution.py:12
  717.3 6.3 collective-permute-start
  723.6 22.0 %collective-permute-start = (bf16[64,1024]{1,0:T(8,128)(2,1)S(1)}, bf16[64,1024]{1,0:T(8,128)(2,1)S(1)}, u32[]{:S(2)}, u32[]{:S(2)}) collective-permute-start(bf16[64,1024]{1,0:T(8,128)(2,1)S(1)} %get-tuple-element.654), channel_id=1, source_target_pairs={{16,0},{32,16},{48,32},{64,48},{80,64},{96,80},{112,96},{128,112},... | collective-permute-start | bytes 393224 | tf_op jit(solution)/shard_map/while/body/eval_jaxpr/ppermute | solution.py:12
  745.6 8.4 collective-permute-start
  754.1 13.1 %collective-permute-start = (bf16[64,1024]{1,0:T(8,128)(2,1)S(1)}, bf16[64,1024]{1,0:T(8,128)(2,1)S(1)}, u32[]{:S(2)}, u32[]{:S(2)}) collective-permute-start(bf16[64,1024]{1,0:T(8,128)(2,1)S(1)} %get-tuple-element.654), channel_id=1, source_target_pairs={{16,0},{32,16},{48,32},{64,48},{80,64},{96,80},{112,96},{128,112},... | collective-permute-start | bytes 393224 | tf_op jit(solution)/shard_map/while/body/eval_jaxpr/ppermute | solution.py:12
  767.2 8.4 collective-permute-start
  (2 other events, 11.6 us)
Sparse Core Ops, SparseCore 0:
  10.0 82.3 all-gather.4
  94.5 74.4 all-gather.2
  780.0 159.0 reduce-scatter.1
where the time goes:
time: 947 us; the launch traced here: 946 us
  waiting for transfers between devices  657 us (69%)
  starting transfers between devices  176 us (19%)
  matrix products  54.8 us (6%)
  blocking collectives  29.2 us (3%)
  between operations  13.8 us (1%)
  other arithmetic  12.6 us (1%)
    ppermute x35, waiting for transfers between devices, passed_along(): return lax.ppermute(block, axis, route)  367 us
    ppermute x35, starting transfers between devices, passed_along(): return lax.ppermute(block, axis, route)  176 us
    reduce_scatter x1, waiting for transfers between devices, shards(): lax.psum_scatter(partial_grad, 'dp', scatter_dimension=0, tiled=True)  130 us
    all_gather x1, waiting for transfers between devices, shards(): lax.all_gather(up_weights, 'dp', axis=1, tiled=True)  81.8 us
    all_gather x1, waiting for transfers between devices, shards(): lax.all_gather(down_weights, 'dp', axis=1, tiled=True)  76.5 us
    psum x1, blocking collectives, shards(): gain_total, scale_total = lax.psum((acc_gain, acc_scale), 'dp')  29.2 us
    dot_general x4, matrix products, layer_back(): jnp.dot(hidden_grad, up_weight.T, preferred_element_type=jnp.float32)  25.3 us
  transfers between devices with their start and end apart: 38, of which 38 were waited for; matrix products, arithmetic and copies ran while one was open for 0% of the time, Pallas kernels for 0%

commit v1 on v0

v1 whole, which is shorter than its diff:
```python
import functools

import jax
import jax.numpy as jnp
from jax import lax
from jax.experimental import pallas as pl
from jax.experimental.pallas import tpu as pltpu
from jax.sharding import PartitionSpec as P

EPSILON = 1e-06
ROOT = 0.7978845608028654
CUBIC = 0.044715
PIECES = 5
CHUNKS = 4
F_TILE = 512
LAG = 2
MESH = pl.DeviceIdType.MESH
NT = (((1,), (1,)), ((), ()))
F32 = jnp.float32
BF16 = jnp.bfloat16


def kernel(
    stages,
    ring,
    len_ref,
    up_ref,
    down_ref,
    x_ref,
    cot_ref,
    gain_ref,
    scale_ref,
    out_ref,
    gain_out,
    scale_out,
    up_w,
    down_w,
    hidden,
    slope,
    act,
    act_t,
    unit,
    inverse,
    normed,
    branch,
    start,
    g_in,
    back,
    bg,
    hg,
    gain_acc,
    stats,
    rs_send_a,
    rs_recv_a,
    rs_send_b,
    rs_recv_b,
    up_sems,
    down_sems,
    chain_sems,
    rs_sems,
    stat_sems,
):
    s = lax.axis_index("pipe")
    z = lax.axis_index("dp")
    last = stages - 1
    right = lax.rem(z + 1, ring)
    left = lax.rem(z + ring - 1, ring)
    above = lax.rem(s + 1, stages)
    below = lax.rem(s + stages - 1, stages)
    width, ff = up_w.shape
    up_rows = up_ref.shape[1]
    down_rows = down_ref.shape[1]
    tokens = normed.shape[0]
    slot = x_ref.shape[1] // 2
    hops_a = ring // 2
    hops_b = ring - 1 - hops_a
    piece_rows = tokens // PIECES
    chunk = width // CHUNKS

    barrier = pltpu.get_barrier_semaphore()
    for place in ({"dp": right}, {"dp": left}, {"pipe": above}, {"pipe": below}):
        pl.semaphore_signal(barrier, inc=1, device_id=place, device_id_type=MESH)
    pl.semaphore_wait(barrier, 4)

    def shard(buffer, rows, owner):
        return buffer.at[pl.ds(pl.multiple_of(owner * rows, rows), rows)]

    def gather_copy(buffer, rows, sems, way, step, first=None):
        owner = lax.rem(z - step + ring, ring) if way == 0 else lax.rem(z + step, ring)
        block = shard(buffer, rows, owner)
        return pltpu.make_async_remote_copy(
            src_ref=block if first is None else first,
            dst_ref=block,
            send_sem=sems.at[0, way, step],
            recv_sem=sems.at[1, way, step],
            device_id={"dp": right if way == 0 else left},
            device_id_type=MESH,
        )

    def gather_arrival(buffer, rows, sems, way, step):
        owner = lax.rem(z - 1 - step + ring, ring) if way == 0 else lax.rem(z + 1 + step, ring)
        block = shard(buffer, rows, owner)
        return pltpu.make_async_remote_copy(
            src_ref=block,
            dst_ref=block,
            send_sem=sems.at[0, way, step],
            recv_sem=sems.at[1, way, step],
            device_id={"dp": right if way == 0 else left},
            device_id_type=MESH,
        )

    weights = (
        (up_w, up_rows, up_sems, up_ref.at[0]),
        (down_w, down_rows, down_sems, down_ref.at[0]),
    )

    def gather_step(which, step):
        buffer, rows, sems, own = weights[which]
        for way, hops in ((0, hops_a), (1, hops_b)):
            if step > 0 and step <= hops:
                gather_arrival(buffer, rows, sems, way, step - 1).wait_recv()
            if step < hops:
                gather_copy(
                    buffer, rows, sems, way, step, own if step == 0 else None
                ).start()

    gather_step(0, 0)
    for buffer, rows, sems, own in weights:
        shard(buffer, rows, z)[...] = own[...]

    first_len = len_ref[0, 0]
    row = lax.broadcasted_iota(jnp.int32, (tokens, x_ref.shape[1]), 0)
    col = lax.broadcasted_iota(jnp.int32, (tokens, x_ref.shape[1]), 1)
    source = jnp.where(row < first_len, row, row + (slot - first_len))
    pick = (col == source).astype(F32).astype(BF16)
    x_rows = jnp.dot(pick, x_ref[0], preferred_element_type=F32)
    scaled = lax.rsqrt(jnp.mean(x_rows * x_rows, axis=-1, keepdims=True) + EPSILON)
    inverse[...] = jnp.broadcast_to(scaled, inverse.shape)
    unit_rows = x_rows * scaled
    unit[...] = unit_rows
    normed[...] = (unit_rows * gain_ref[...]).astype(BF16)
    start[...] = jnp.dot(pick, cot_ref[...], preferred_element_type=F32).astype(BF16)
    gain_acc[...] = jnp.zeros_like(gain_acc)

    def hidden_tile(tile):
        cols = pl.ds(pl.multiple_of(tile * F_TILE, F_TILE), F_TILE)
        h = jnp.dot(normed[...], up_w[:, cols], preferred_element_type=F32)
        square = h * h
        th = jnp.tanh(ROOT * (h + CUBIC * (square * h)))
        half = 0.5 * (1.0 + th)
        a = h * half
        hidden[:, cols] = h
        slope[:, cols] = half + 0.5 * h * (1.0 - th * th) * (
            ROOT * (1.0 + (3.0 * CUBIC) * square)
        )
        act[:, cols] = a.astype(BF16)
        act_t[cols, :] = a.T.astype(BF16)

    tiles = ff // F_TILE
    for step in range(1, hops_a + LAG + 1):
        if step <= hops_a:
            gather_step(0, step)
        if step >= LAG:
            gather_step(1, step - LAG)
        if step >= hops_a and step < hops_a + LAG:
            part = step - hops_a
            lax.fori_loop(
                part * tiles // LAG,
                (part + 1) * tiles // LAG,
                lambda tile, c: (hidden_tile(tile), c)[1],
                0,
            )

    @pl.when(s == last)
    def _():
        for c in range(CHUNKS):
            g_in[c] = start[:, c * chunk : (c + 1) * chunk]

    def branch_tile(tile, carry):
        cols = pl.ds(pl.multiple_of(tile * F_TILE, F_TILE), F_TILE)
        branch[:, cols] = jnp.dot(act[...], down_w[:, cols], preferred_element_type=F32)
        return carry

    @pl.when(s < last)
    def _():
        lax.fori_loop(0, width // F_TILE, branch_tile, 0)

    def chain_copy(p, c):
        rows = pl.ds(pl.multiple_of(p * piece_rows, piece_rows), piece_rows)
        return pltpu.make_async_remote_copy(
            src_ref=back.at[c, rows],
            dst_ref=g_in.at[c, rows],
            send_sem=chain_sems.at[0, p, c],
            recv_sem=chain_sems.at[1, p, c],
            device_id={"pipe": below},
            device_id_type=MESH,
        )

    def piece(p, carry):
        rows = pl.ds(pl.multiple_of(p * piece_rows, piece_rows), piece_rows)
        for c in range(CHUNKS):

            @pl.when(s < last)
            def _():
                chain_copy(p, c).wait_recv()

            cols = slice(c * chunk, (c + 1) * chunk)
            bg[rows, cols] = (g_in[c, rows].astype(F32) * scale_ref[:, cols]).astype(BF16)
        grad = bg[rows, :]
        total = jnp.zeros((piece_rows, 1), F32)
        for f in range(tiles):
            cols = slice(f * F_TILE, (f + 1) * F_TILE)
            act_grad = lax.dot_general(grad, down_w[cols, :], NT, preferred_element_type=F32)
            rounded = (act_grad * slope[rows, cols]).astype(BF16)
            hg[rows, cols] = rounded
            total += jnp.sum(rounded.astype(F32) * hidden[rows, cols], axis=-1, keepdims=True)
        mean = total * (1.0 / width)
        inv = inverse[rows, 0:1]
        hidden_grad = hg[rows, :]
        for c in range(CHUNKS):
            cols = slice(c * chunk, (c + 1) * chunk)
            normed_grad = lax.dot_general(
                hidden_grad, up_w[cols, :], NT, preferred_element_type=F32
            )
            unit_part = unit[rows, cols]
            back[c, rows] = (
                g_in[c, rows].astype(F32)
                + inv * (normed_grad * gain_ref[:, cols] - unit_part * mean)
            ).astype(BF16)

            @pl.when(s > 0)
            def _():
                chain_copy(p, c).start()

            gain_acc[:, cols] += jnp.sum(normed_grad * unit_part, axis=0, keepdims=True)
        return carry

    lax.fori_loop(0, PIECES, piece, 0)

    @pl.when(s == last)
    def _():
        lax.fori_loop(0, width // F_TILE, branch_tile, 0)

    stats[z, 0:1, :] = gain_acc[...]
    for c in range(CHUNKS):
        cols = slice(c * chunk, (c + 1) * chunk)
        stats[z, 1:2, cols] = jnp.sum(
            g_in[c].astype(F32) * branch[:, cols], axis=0, keepdims=True
        )

    def own_part(dest):
        rows = pl.ds(pl.multiple_of(dest * down_rows, down_rows), down_rows)
        return jnp.dot(act_t[rows, :], bg[...], preferred_element_type=F32)

    ways = (
        (0, hops_a, rs_send_a, rs_recv_a, right),
        (1, hops_b, rs_send_b, rs_recv_b, left),
    )

    def rs_copy(way, j):
        number, hops, sent, received, target = ways[way]
        return pltpu.make_async_remote_copy(
            src_ref=sent.at[j],
            dst_ref=received.at[j],
            send_sem=rs_sems.at[0, way, j],
            recv_sem=rs_sems.at[1, way, j],
            device_id={"dp": target},
            device_id_type=MESH,
        )

    def stat_copy(way, j, arrival=False):
        ahead = j + 1 if arrival else j
        owner = lax.rem(z - ahead + ring, ring) if way == 0 else lax.rem(z + ahead, ring)
        return pltpu.make_async_remote_copy(
            src_ref=stats.at[owner],
            dst_ref=stats.at[owner],
            send_sem=stat_sems.at[0, way, j],
            recv_sem=stat_sems.at[1, way, j],
            device_id={"dp": right if way == 0 else left},
            device_id_type=MESH,
        )

    def rs_step(j, carry):
        for way, hops, sent, received, target in ways:

            @pl.when(j < hops)
            def _():
                ahead = hops - j
                dest = lax.rem(z + ahead, ring) if way == 0 else lax.rem(z - ahead + ring, ring)
                value = own_part(dest)

                @pl.when(j == 0)
                def _():
                    sent[j] = value.astype(BF16)

                @pl.when(j > 0)
                def _():
                    rs_copy(way, j - 1).wait_recv()
                    sent[j] = (value + received[j - 1].astype(F32)).astype(BF16)

                rs_copy(way, j).start()

                @pl.when(j > 0)
                def _():
                    stat_copy(way, j - 1, True).wait_recv()

                stat_copy(way, j).start()

        return carry

    lax.fori_loop(0, hops_a, rs_step, 0)
    value = own_part(z)
    for way, hops, sent, received, target in ways:
        rs_copy(way, hops - 1).wait_recv()
        value = value + received[hops - 1].astype(F32)
        stat_copy(way, hops - 1, True).wait_recv()
    out_ref[0] = value.astype(BF16)
    summed = stats[0]
    for i in range(1, ring):
        summed = summed + stats[i]
    gain_out[...] = summed[0:1]
    scale_out[...] = summed[1:2]

    for way, hops in ((0, hops_a), (1, hops_b)):
        for step in range(hops):
            for buffer, rows, sems, own in weights:
                gather_copy(
                    buffer, rows, sems, way, step, own if step == 0 else None
                ).wait_send()
            rs_copy(way, step).wait_send()
            stat_copy(way, step).wait_send()

    @pl.when(s > 0)
    def _():
        for p in range(PIECES):
            for c in range(CHUNKS):
                chain_copy(p, c).wait_send()


def shards(stages, ring, x_saved, up_weights, down_weights, norm_gain, layer_scale, cotangent, lengths):
    unused, rows, width = x_saved.shape
    ff = up_weights.shape[2]
    down_rows = down_weights.shape[1]
    tokens = rows * 5 // 8
    hops_a = ring // 2
    hops_b = ring - 1 - hops_a
    vmem = pl.BlockSpec(memory_space=pltpu.VMEM)
    smem = pl.BlockSpec(memory_space=pltpu.SMEM)
    return pl.pallas_call(
        functools.partial(kernel, stages, ring),
        out_shape=(
            jax.ShapeDtypeStruct((1, down_rows, width), BF16),
            jax.ShapeDtypeStruct((1, width), F32),
            jax.ShapeDtypeStruct((1, width), F32),
        ),
        in_specs=[smem] + [vmem] * 6,
        out_specs=(vmem, vmem, vmem),
        scratch_shapes=[
            pltpu.VMEM((width, ff), BF16),
            pltpu.VMEM((ff, width), BF16),
            pltpu.VMEM((tokens, ff), F32),
            pltpu.VMEM((tokens, ff), F32),
            pltpu.VMEM((tokens, ff), BF16),
            pltpu.VMEM((ff, tokens), BF16),
            pltpu.VMEM((tokens, width), F32),
            pltpu.VMEM((tokens, 128), F32),
            pltpu.VMEM((tokens, width), BF16),
            pltpu.VMEM((tokens, width), F32),
            pltpu.VMEM((tokens, width), BF16),
            pltpu.VMEM((CHUNKS, tokens, width // CHUNKS), BF16),
            pltpu.VMEM((CHUNKS, tokens, width // CHUNKS), BF16),
            pltpu.VMEM((tokens, width), BF16),
            pltpu.VMEM((tokens, ff), BF16),
            pltpu.VMEM((1, width), F32),
            pltpu.VMEM((ring, 2, width), F32),
            pltpu.VMEM((hops_a, down_rows, width), BF16),
            pltpu.VMEM((hops_a, down_rows, width), BF16),
            pltpu.VMEM((hops_b, down_rows, width), BF16),
            pltpu.VMEM((hops_b, down_rows, width), BF16),
            pltpu.SemaphoreType.DMA((2, 2, hops_a)),
            pltpu.SemaphoreType.DMA((2, 2, hops_a)),
            pltpu.SemaphoreType.DMA((2, PIECES, CHUNKS)),
            pltpu.SemaphoreType.DMA((2, 2, hops_a)),
            pltpu.SemaphoreType.DMA((2, 2, hops_a)),
        ],
        compiler_params=pltpu.CompilerParams(
            collective_id=0, has_side_effects=True, vmem_limit_bytes=60 * 1024 * 1024
        ),
        name="layer_chain",
    )(lengths, up_weights, down_weights, x_saved, cotangent, norm_gain, layer_scale)


def solution(mesh):
    return jax.shard_map(
        functools.partial(shards, mesh.shape["pipe"], mesh.shape["dp"]),
        mesh=mesh,
        in_specs=(
            P("pipe", "dp", None),
            P("pipe", "dp", None),
            P("pipe", "dp", None),
            P("pipe", None),
            P("pipe", None),
            P("dp", None),
            P("dp", None),
        ),
        out_specs=(P("pipe", "dp", None), P("pipe", None), P("pipe", None)),
        check_vma=False,
    )
```

time: 947 us -> 358 us (0.38)
  the two profiles are of different devices: /device:TPU:12 before, /device:TPU:96 now
where the time goes in v1:
time: 358 us
  Pallas kernels  354 us (99%)
    pallas_call x1, Pallas kernels, shards(): pl.pallas_call(functools.partial(kernel, stages, ring), out_shape=(jax.Sh...  354 us

profile of v1, /device:TPU:96, one launch (start us, length us, event | category | flops | bytes accessed | tf_op | source)
XLA Modules:
  0.0 357.7 jit_solution(603840060353751443)
XLA Ops:
  0.6 354.1 %layer_chain.1 = (bf16[1,128,1024]{2,1,0:T(8,128)(2,1)}, f32[1,1024]{1,0:T(1,128)}, f32[1,1024]{1,0:T(1,128)}) custom-call(s32[1,2]{1,0:T(1,128)} %len_ref.1, bf16[1,64,2048]{2,1,0:T(8,128)(2,1)} %up_ref.1, bf16[1,128,1024]{2,1,0:T(8,128)(2,1)} %down_ref.1, bf16[1,256,1024]{2,1,0:T(8,128)(2,1)} %x_ref.1, bf16[256,1024]{1,0:T(8,128)(2,1)} %cot_ref.1, ...), custom_call_target="tpu_custom_call" | custom-call | tf_op jit(solution)/shard_map/layer_chain/pallas_call | solution.py:349
  354.7 0.0 copy-start.1
  354.8 1.7 copy.13
  356.4 0.0 copy-done.1
  356.4 0.0 copy-start
  356.4 0.6 copy.14
  357.0 0.1 copy-done
  357.1 0.6 copy.15
Async XLA Ops:
  354.7 1.7 copy-start.1
  356.4 0.7 copy-start
